TPU v7x, 256 devices: a whole 4x4x8 slice. The times are simulated.
256 devices in a mesh: lat: 8 (over y, x_hi), lon: 32 (over z, x_lo, core).
Axes of the slice: x: 4 (x_hi: 2, x_lo: 2; x = x_hi * 2 + x_lo), y: 4, z: 8, core: 2. Of those that a mesh axis runs over, the one named last changes fastest.
Arguments:
- features: bfloat16 [256, 4096, 128], P('lat', 'lon'), may hold values from -6 to 6
- land_mask: int32 [256, 4096], P('lat', 'lon'), may hold values 0 or 1
- dw_weight: float32 [7, 7, 128], replicated, may hold values from -0.875 to 0.875
- dw_bias: float32 [128], replicated, may hold values from -3 to 3
- norm_gain: float32 [128], replicated, may hold values from 0.25 to 1.75
- norm_shift: float32 [128], replicated, may hold values from -3 to 3
- expand_weight: bfloat16 [128, 512], replicated, may hold values from -0.5 to 0.5
- expand_bias: float32 [512], replicated, may hold values from -3 to 3
- project_weight: bfloat16 [512, 128], replicated, may hold values from -0.25 to 0.25
- project_bias: float32 [128], replicated, may hold values from -3 to 3
- layer_scale: float32 [128], replicated, may hold values from 0.3 to 1
- out_gain: float32 [128], replicated, may hold values from 0.25 to 1.75
- out_shift: float32 [128], replicated, may hold values from -3 to 3
- coarse_weight: bfloat16 [4, 4, 128, 256], replicated, may hold values from -0.125 to 0.125
- coarse_bias: float32 [256], replicated, may hold values from -3 to 3
Outputs:
- coarse: bfloat16 [128, 2048, 256], P('lat', 'lon')
All inputs are finite; a program needn't handle non-finite values. No bound on the sum of `land_mask` on one device may be relied on, other than what follows from the above.
Results may differ from a plain program's by a relative error of at most 0.0051.
Values may be sent and summed in bfloat16 or wider, within the bound.
No kernel may reach another device: no remote copies, remote signals or barrier semaphores. Data moves between devices by JAX's collectives and lax.ppermute only.
A program may use at most 64 MiB of HBM per device.

v0:
```python
import jax
import jax.numpy as jnp
from jax import lax
from jax.experimental import pallas as pl
from jax.experimental.pallas import tpu as pltpu
from jax.sharding import PartitionSpec as P


F32 = jnp.float32
BF16 = jnp.bfloat16
RIM = 4
LEFT = 8
SIZE = 7
SPAN = 144
GROUP = 4


def dot(a, b):
    return jnp.dot(a, b, preferred_element_type=F32)


def spread_rows(field, shifted, count, chan):
    @pl.loop(0, count)
    def _(p):
        for b in range(SIZE):
            for g in range(2):
                lane = (2 * b + g) * chan
                start = b + LEFT - RIM
                shifted[p, :, lane : lane + chan] = field[2 * p + g, start : start + SPAN].astype(
                    BF16
                )


def centring(chan):
    square = (chan, chan)
    same = lax.broadcasted_iota(jnp.int32, square, 0) == lax.broadcasted_iota(jnp.int32, square, 1)
    return jnp.where(same, F32(1.0), F32(0.0)) - F32(1.0 / chan)


def build_taps(dw, taps, finished):
    chan = dw.shape[2]
    matrix = centring(chan)
    nothing = jnp.zeros((chan, chan), BF16)
    for a in range(-1, SIZE + 1):
        for b in range(SIZE):
            if 0 <= a < SIZE:
                block = (matrix * dw[a, b : b + 1]).astype(BF16)
            else:
                block = nothing
            for h in range(2):
                k, g = divmod(a + h, 2)
                if 0 <= a + h <= SIZE:
                    place = ((k * SIZE + b) * 2 + g) * chan
                    taps[h * chan : (h + 1) * chan, place : place + chan] = block
        if a >= 0 and a % 2 == 1:
            finished(a // 2)


def conv(shifted, starts, taps):
    chan2 = taps.shape[0]
    rhs = taps[...]
    totals = []
    for start in starts:
        lhs = [
            shifted[pl.ds(start + k, 2)].reshape(2 * SPAN, SIZE * chan2) for k in range(4)
        ]
        totals.append(
            lax.dot_general(
                jnp.concatenate(lhs, axis=1),
                rhs,
                (((1,), (1,)), ((), ())),
                preferred_element_type=F32,
            )
        )
    return totals


def average_of(chan):
    both = (2 * chan, 2 * chan)
    row_id = lax.broadcasted_iota(jnp.int32, both, 0)
    col_id = lax.broadcasted_iota(jnp.int32, both, 1)
    return jnp.where(
        (row_id < chan) == (col_id < chan), F32(1.0 / chan), F32(0.0)
    ).astype(BF16)


def two(vector):
    return jnp.concatenate([vector, vector], axis=1)


def centred_row(vector):
    return vector - jnp.mean(vector, axis=-1, keepdims=True)


def cells(streams, refs, norm_buf, coarse_in, average):
    chan = average.shape[0] // 2
    marks, norm_gain, norm_shift, expand, expand_bias, project, project_bias, out_gain, out_shift = refs
    half = coarse_in.shape[1]
    mark_row = lax.broadcasted_iota(jnp.int32, (chan, chan), 0)
    table = marks[...].astype(BF16)
    centred = [s[0] for s in streams]
    spread = [dot((c * c).astype(BF16), average) for c in centred]
    gain, shift = two(norm_gain[...]), two(norm_shift[...])
    normed = [
        (c * lax.rsqrt(v + 1e-06) * gain + shift).astype(BF16) for c, v in zip(centred, spread)
    ]
    parts = [[] for _ in streams]
    for h in range(2):
        for i, s in enumerate(streams):
            pre = dot(normed[i][:, h * chan : (h + 1) * chan], expand[...]) + expand_bias[...]
            hidden = (pre * (1.0 + lax.erf(pre * (0.5**0.5)))).astype(BF16)
            parts[i].append(dot(jnp.concatenate([hidden, s[1][h]], axis=1), project[...]))
    bias = two(project_bias[...])
    updated = [jnp.concatenate(p, axis=1) + bias for p in parts]
    spread = [dot((u * u).astype(BF16), average) for u in updated]
    gain, shift = two(out_gain[...]), two(out_shift[...])
    for i, s in enumerate(streams):
        mark = []
        for rows_of in s[2]:
            chosen = jnp.concatenate(
                [(mark_row == r).astype(F32).astype(BF16) for r in rows_of], axis=1
            )
            mark.append(dot(table, chosen))
        mark = jnp.concatenate(mark, axis=0)
        normalized = mark * (updated[i] * lax.rsqrt(spread[i] + 1e-06) * gain + shift)
        for j, slot in enumerate(s[3]):
            for h in range(2):
                buf = norm_buf.at[s[4] + j, h]
                buf[...] = normalized[j * SPAN : (j + 1) * SPAN, h * chan : (h + 1) * chan]
                for b in range(4):
                    lane = (2 * b + h) * chan
                    coarse_in[slot, :, lane : lane + chan] = buf[
                        pl.ds(b, half, stride=2), :
                    ].astype(BF16)


def coarse_rows(coarse_in, first, count, coarse_w, coarse_b):
    total = coarse_b[...]
    for k in range(2):
        kernel = jnp.concatenate(
            [coarse_w[2 * k + h, b] for b in range(4) for h in range(2)], axis=0
        )
        window = coarse_in[first + k : first + k + count]
        total = total + dot(window.reshape(-1, window.shape[2]), kernel)
    return total.astype(BF16).reshape(count, coarse_in.shape[1], -1)


def own_cells(shifted, at, mid, chan):
    return [
        shifted[
            pl.ds(at + 1 + h, 2), :, mid + (1 - h) * chan : mid + (2 - h) * chan
        ].reshape(2 * SPAN, chan)
        for h in range(2)
    ]


def prepare_kernel(dw, project_w, layer_scale, taps_hbm, project, taps, sems):
    hid, chan = project_w.shape
    depth = taps.shape[1] // 4

    def piece(k):
        cut = slice(k * depth, (k + 1) * depth)
        return pltpu.make_async_copy(taps.at[:, cut], taps_hbm.at[:, cut], sems.at[k])

    build_taps(dw, taps, lambda k: piece(k).start())
    scaled = project_w[...].astype(F32) * layer_scale[...]
    project[:hid] = (0.5 * centred_row(scaled)).astype(BF16)
    project[hid:] = centring(chan).astype(BF16)
    for k in range(4):
        piece(k).wait()


def inner_kernel(
    feat,
    west,
    east,
    land_mask,
    dw_bias,
    norm_gain,
    norm_shift,
    expand,
    expand_bias,
    project,
    project_b,
    layer_scale,
    out_gain,
    out_shift,
    coarse_b,
    taps_hbm,
    coarse_w_hbm,
    out,
    edges,
    field,
    shifted,
    norm_buf,
    coarse_in,
    marks,
    project_bias,
    conv_buf,
    taps,
    coarse_w,
    sems,
):
    rows, cols, chan = feat.shape
    load_taps = pltpu.make_async_copy(taps_hbm, taps, sems.at[0])
    load_coarse = pltpu.make_async_copy(coarse_w_hbm, coarse_w, sems.at[1])
    load_taps.start()
    load_coarse.start()
    field[:, : LEFT - RIM] = jnp.zeros((rows, LEFT - RIM, chan), F32)
    field[:, LEFT + cols + RIM :] = jnp.zeros((rows, SPAN + 16 - LEFT - cols - RIM, chan), F32)
    field[:, LEFT : LEFT + cols] = feat[...].astype(F32)
    field[:, LEFT - RIM : LEFT] = west[:rows].astype(F32)
    field[:, LEFT + cols : LEFT + cols + RIM] = east[:rows].astype(F32)
    count = shifted.shape[0]
    spread_rows(field, shifted, count, chan)

    project_bias[...] = centred_row(project_b[...] * layer_scale[...])

    side_table(land_mask, west, east, marks)
    average = average_of(chan)
    bias = two(centred_row(dw_bias[...]))
    refs = (
        marks,
        norm_gain,
        norm_shift,
        expand,
        expand_bias,
        project,
        project_bias,
        out_gain,
        out_shift,
    )
    mid = (SIZE // 2) * 2 * chan

    load_taps.wait()

    @pl.loop(0, (count - 3) // GROUP)
    def _(group):
        base = group * GROUP
        streams = []

        @pl.when(group >= 0)
        def _():
            for i, total in enumerate(conv(shifted, [base, base + 2], taps)):
                conv_buf[i] = total + bias

        for i in range(2):
            slot = base + 2 * i
            top = 2 * (slot + 2)
            streams.append(
                (
                    conv_buf[i],
                    own_cells(shifted, slot, mid, chan),
                    [(top - 1, top), (top + 1, top + 2)],
                    [slot, slot + 1],
                    2 * i,
                )
            )
        cells(streams, refs, norm_buf, coarse_in, average)

    done = coarse_in.shape[0] - 1
    load_coarse.wait()
    for first in range(0, done, 4):
        size = min(4, done - first)
        out[2 + first : 2 + first + size] = coarse_rows(coarse_in, first, size, coarse_w, coarse_b)
    edges[0] = coarse_in[0]
    edges[1] = coarse_in[done]


def side_table(land_mask, west, east, marks):
    rows, cols = land_mask.shape

    def neighbour(packed):
        lines = [packed[rows + m] for m in range(rows // RIM)]
        return jnp.concatenate([line.astype(F32) for line in lines], axis=0)

    def turned(block):
        return jnp.concatenate([block, jnp.zeros((cols - rows, cols), F32)], axis=0).T

    own = turned(land_mask[...].astype(F32))
    left = turned(neighbour(west))
    right = turned(neighbour(east))
    marks[cols:, :] = jnp.zeros((SPAN - cols, cols), F32)
    marks[1 : cols + 1, :] = own
    marks[0:1, :] = left[cols - 1 : cols]
    marks[cols + 1 : cols + 2, :] = right[0:1]


def rim_kernel(lat, feat_low, feat_high, west, east, land_mask, swap_a, swap_b, block):
    rows, cols = land_mask.shape
    chan = feat_low.shape[2]
    parity = lat[0] % 2
    deep = lax.broadcasted_iota(jnp.int32, (SPAN, cols), 1)
    place = lax.broadcasted_iota(jnp.int32, (SPAN, cols), 0)
    ones = jnp.ones((cols, chan), BF16)

    def fill(feat, first, row):
        block[:RIM, RIM : RIM + cols] = feat[...].astype(F32)
        block[:RIM, :RIM] = west[first : first + RIM].astype(F32)
        block[:RIM, RIM + cols : 2 * RIM + cols] = east[first : first + RIM].astype(F32)
        block[:RIM, 2 * RIM + cols :] = jnp.zeros((RIM, SPAN - 2 * RIM - cols, chan), F32)
        at, part = divmod(row, RIM)
        left = west[rows + at].astype(F32)[part : part + 1]
        right = east[rows + at].astype(F32)[part : part + 1]
        line = land_mask[row : row + 1].astype(F32)
        zero = jnp.zeros((SPAN, cols), F32)
        table = (
            jnp.where(deep == place - RIM, line, zero)
            + jnp.where((place == RIM - 1) & (deep == cols - 1), left, zero)
            + jnp.where((place == RIM + cols) & (deep == 0), right, zero)
        )
        block[RIM] = dot(table.astype(BF16), ones)

    fill(feat_high, rows - RIM, rows - 1)

    @pl.when(parity == 0)
    def _():
        swap_a[...] = block[...].astype(BF16)

    @pl.when(parity == 1)
    def _():
        swap_b[...] = block[...].astype(BF16)

    @pl.when(lat[0] == lat[1])
    def _():
        width = cols + 2 * RIM
        wide = (SPAN, SPAN)
        total = lax.broadcasted_iota(jnp.int32, wide, 0) + lax.broadcasted_iota(jnp.int32, wide, 1)
        turn = (total == width - 1).astype(F32).astype(BF16)
        for r in range(RIM + 1):
            source = RIM - 1 - r if r < RIM else r
            swap_b[r] = dot(turn, block[source].astype(BF16)).astype(BF16)

    fill(feat_low, 0, 0)

    @pl.when(parity == 0)
    def _():
        swap_b[...] = block[...].astype(BF16)

    @pl.when(parity == 1)
    def _():
        swap_a[...] = block[...].astype(BF16)


def outer_kernel(
    lat,
    feat_low,
    feat_high,
    west,
    east,
    rim_a,
    rim_b,
    land_mask,
    dw,
    dw_bias,
    norm_gain,
    norm_shift,
    expand,
    expand_bias,
    project_b,
    layer_scale,
    out_gain,
    out_shift,
    coarse_b,
    project,
    taps_hbm,
    edges_hbm,
    coarse_w_hbm,
    whole_in,
    whole,
    field,
    shifted,
    last_buf,
    norm_buf,
    coarse_in,
    marks,
    taps,
    coarse_w,
    edges,
    project_bias,
    out_buf,
    conv_buf,
    sems,
):
    del whole_in
    load_taps = pltpu.make_async_copy(taps_hbm, taps, sems.at[0])
    load_edges = pltpu.make_async_copy(edges_hbm, edges, sems.at[2])
    load_coarse = pltpu.make_async_copy(coarse_w_hbm, coarse_w, sems.at[1])
    load_taps.start()
    load_edges.start()
    load_coarse.start()
    project_bias[...] = centred_row(project_b[...] * layer_scale[...])
    chan = feat_low.shape[2]
    rows, cols = land_mask.shape
    low = 6
    high = RIM + low
    top = high + 8
    used = top + RIM
    left, right = LEFT - RIM, LEFT + cols + RIM
    field[:, :left] = jnp.zeros((used + 2, left, chan), F32)
    field[:, right:] = jnp.zeros((used + 2, SPAN + 16 - right, chan), F32)

    def place(south, north):
        field[:RIM, left:right] = south[:RIM, : right - left].astype(F32)
        field[top:used, left:right] = north[:RIM, : right - left].astype(F32)
        field[used, left:right] = north[RIM, : right - left].astype(F32)
        field[used + 1, left:right] = south[RIM, : right - left].astype(F32)

    @pl.when(lat[0] % 2 == 0)
    def _():
        place(rim_b, rim_a)

    @pl.when(lat[0] % 2 == 1)
    def _():
        place(rim_a, rim_b)

    @pl.when(lat[0] == 0)
    def _():
        field[:RIM, left:right] = jnp.zeros((RIM, right - left, chan), F32)
        field[used + 1, left:right] = jnp.zeros((right - left, chan), F32)

    field[RIM:high, LEFT : LEFT + cols] = feat_low[:low].astype(F32)
    field[RIM:high, left:LEFT] = west[:low].astype(F32)
    field[RIM:high, LEFT + cols : right] = east[:low].astype(F32)
    field[high:top, LEFT : LEFT + cols] = feat_high[...].astype(F32)
    field[high:top, left:LEFT] = west[rows - 8 : rows].astype(F32)
    field[high:top, LEFT + cols : right] = east[rows - 8 : rows].astype(F32)

    side_table(land_mask, west, east, marks)
    lane = lax.broadcasted_iota(jnp.int32, (SPAN, chan), 1)
    start = LEFT - 1
    table = jnp.where(lane == rows, field[used, start : start + SPAN], marks[...])
    marks[...] = jnp.where(lane == rows + 1, field[used + 1, start : start + SPAN], table)
    spread_rows(field, shifted, shifted.shape[0], chan)

    average = average_of(chan)
    bias = two(centred_row(dw_bias[...]))
    refs = (
        marks,
        norm_gain,
        norm_shift,
        expand,
        expand_bias,
        project,
        project_bias,
        out_gain,
        out_shift,
    )
    mid = (SIZE // 2) * 2 * chan
    part = SPAN // 2
    first_row = high + 4
    turned = lat[0] == lat[1]
    for n in range(0, SPAN, part):
        accs = [jnp.zeros((part, chan), F32) + dw_bias[...] for _ in range(2)]
        for r in range(SIZE + 1):
            for b in range(SIZE):
                start = n + b + left
                piece = field[first_row + r, start : start + part]
                if r < SIZE:
                    accs[0] = accs[0] + piece * dw[r, b : b + 1]
                if r > 0:
                    weight = jnp.where(
                        turned,
                        dw[SIZE - r, SIZE - 1 - b : SIZE - b],
                        dw[r - 1, b : b + 1],
                    )
                    accs[1] = accs[1] + piece * weight
        for h in range(2):
            last_buf[n : n + part, h * chan : (h + 1) * chan] = centred_row(accs[h])

    load_taps.wait()
    load_edges.wait()
    coarse_in[2] = edges[0]
    coarse_in[3] = edges[1]

    @pl.when(lat[0] >= 0)
    def _():
        for i, total in enumerate(conv(shifted, [0, 5], taps)):
            conv_buf[i] = total + bias

    start = SIZE // 2 + left
    streams = [
        (
            conv_buf[0],
            own_cells(shifted, 0, mid, chan),
            [(rows + 1, 0), (1, 2)],
            [0, 1],
            0,
        ),
        (
            conv_buf[1],
            own_cells(shifted, 5, mid, chan),
            [(rows - 5, rows - 4), (rows - 3, rows - 2)],
            [4, 5],
            2,
        ),
        (
            last_buf[...],
            [field[first_row + 3 + h, start : start + SPAN].astype(BF16) for h in range(2)],
            [(rows - 1, rows)],
            [6],
            4,
        ),
    ]
    cells(streams, refs, norm_buf, coarse_in, average)
    load_coarse.wait()
    out_buf[:2] = coarse_rows(coarse_in, 0, 2, coarse_w, coarse_b)
    out_buf[2:5] = coarse_rows(coarse_in, 3, 3, coarse_w, coarse_b)
    count = whole.shape[0]
    low_copy = pltpu.make_async_copy(out_buf.at[:2], whole.at[:2], sems.at[0])
    high_copy = pltpu.make_async_copy(out_buf.at[2:5], whole.at[count - 3 : count], sems.at[1])
    low_copy.start()
    high_copy.start()
    low_copy.wait()
    high_copy.wait()


def local(
    features,
    land_mask,
    dw_weight,
    dw_bias,
    norm_gain,
    norm_shift,
    expand_weight,
    expand_bias,
    project_weight,
    project_bias,
    layer_scale,
    out_gain,
    out_shift,
    coarse_weight,
    coarse_bias,
):
    rows, cols, chan = features.shape
    n_lat = lax.axis_size("lat")
    n_lon = lax.axis_size("lon")
    marks = land_mask.astype(BF16)
    extra = marks.reshape(rows // RIM, RIM, cols)
    around = [(i, (i + 1) % n_lon) for i in range(n_lon)]
    back = [(j, i) for i, j in around]
    to_east = jnp.concatenate([features[:, cols - RIM :], extra], axis=0)
    to_west = jnp.concatenate([features[:, :RIM], extra], axis=0)
    west = lax.ppermute(to_east, "lon", around)
    east = lax.ppermute(to_west, "lon", back)
    lat = jnp.stack([lax.axis_index("lat"), jnp.int32(n_lat - 1)])
    last = rows // 8 - 1
    scalars = pl.BlockSpec(memory_space=pltpu.SMEM)
    vmem = pl.BlockSpec(memory_space=pltpu.VMEM)
    hbm = pl.BlockSpec(memory_space=pl.ANY)
    band = jax.ShapeDtypeStruct((RIM + 1, SPAN, chan), BF16)
    swap_a, swap_b = pl.pallas_call(
        rim_kernel,
        out_shape=(band, band),
        in_specs=[scalars] + [vmem] * 5,
        out_specs=(vmem, vmem),
        scratch_shapes=[pltpu.VMEM((RIM + 1, SPAN, chan), F32)],
        compiler_params=pltpu.CompilerParams(vmem_limit_bytes=8000 * 1024),
        name="rims",
    )(lat, features[:RIM], features[rows - RIM :], west, east, land_mask)
    pairs_a = [(i ^ 1, i) for i in range(n_lat)]
    pairs_b = []
    for i in range(n_lat):
        for j in range(n_lon):
            if i == 0:
                to = (0, j)
            elif i == n_lat - 1:
                to = (i, n_lon - 1 - j)
            else:
                to = (((i + 1) ^ 1) - 1, j)
            pairs_b.append((i * n_lon + j, to[0] * n_lon + to[1]))
    rim_a = lax.ppermute(swap_a, "lat", pairs_a)
    rim_b = lax.ppermute(swap_b, ("lat", "lon"), pairs_b)

    hid = expand_weight.shape[1]
    out_count = coarse_weight.shape[3]
    half_cols = cols // 2
    whole_shape = jax.ShapeDtypeStruct((rows // 2, half_cols, out_count), BF16)
    inner_pairs = rows // 2 - GROUP
    norm_gain, norm_shift, expand_bias, project_bias, layer_scale = (
        v[None] for v in (norm_gain, norm_shift, expand_bias, project_bias, layer_scale)
    )
    out_gain, out_shift, coarse_bias, dw_bias = (
        v[None] for v in (out_gain, out_shift, coarse_bias, dw_bias)
    )
    taps_shape = jax.ShapeDtypeStruct((2 * chan, SIZE * 8 * chan), BF16)
    taps, project = pl.pallas_call(
        prepare_kernel,
        out_shape=(taps_shape, jax.ShapeDtypeStruct((hid + chan, chan), BF16)),
        in_specs=[vmem] * 3,
        out_specs=(hbm, vmem),
        scratch_shapes=[
            pltpu.VMEM(taps_shape.shape, BF16),
            pltpu.SemaphoreType.DMA((4,)),
        ],
        compiler_params=pltpu.CompilerParams(vmem_limit_bytes=58 * 1024 * 1024),
        cost_estimate=pl.CostEstimate(
            flops=2_000_000_000, bytes_accessed=4_000_000, transcendentals=0
        ),
        name="prepare",
    )(dw_weight, project_weight, layer_scale)
    operands = (
        features,
        west,
        east,
        land_mask,
        dw_bias,
        norm_gain,
        norm_shift,
        expand_weight,
        expand_bias,
        project,
        project_bias,
        layer_scale,
        out_gain,
        out_shift,
        coarse_bias,
        taps,
        coarse_weight,
    )
    whole, edges = pl.pallas_call(
        inner_kernel,
        out_shape=(whole_shape, jax.ShapeDtypeStruct((2, half_cols, 8 * chan), BF16)),
        in_specs=[vmem] * (len(operands) - 2) + [hbm] * 2,
        out_specs=(vmem,) * 2,
        scratch_shapes=[
            pltpu.VMEM((rows, SPAN + 16, chan), F32),
            pltpu.VMEM((inner_pairs + 3, SPAN, SIZE * 2 * chan), BF16),
            pltpu.VMEM((GROUP, 2, SPAN, chan), F32),
            pltpu.VMEM((inner_pairs, half_cols, 8 * chan), BF16),
            pltpu.VMEM((SPAN, chan), F32),
            pltpu.VMEM((1, chan), F32),
            pltpu.VMEM((2, 2 * SPAN, 2 * chan), F32),
            pltpu.VMEM(taps_shape.shape, BF16),
            pltpu.VMEM(coarse_weight.shape, BF16),
            pltpu.SemaphoreType.DMA((2,)),
        ],
        compiler_params=pltpu.CompilerParams(vmem_limit_bytes=58 * 1024 * 1024),
        cost_estimate=pl.CostEstimate(
            flops=16_000_000_000, bytes_accessed=8_000_000, transcendentals=0
        ),
        name="inner",
    )(*operands)

    operands = (
        lat,
        features,
        features,
        west,
        east,
        rim_a,
        rim_b,
        land_mask,
        dw_weight,
        dw_bias,
        norm_gain,
        norm_shift,
        expand_weight,
        expand_bias,
        project_bias,
        layer_scale,
        out_gain,
        out_shift,
        coarse_bias,
        project,
        taps,
        edges,
        coarse_weight,
        whole,
    )
    specs = [vmem] * (len(operands) - 4) + [hbm] * 4
    specs[0] = scalars
    specs[1] = pl.BlockSpec((8, cols, chan), lambda i: (0, 0, 0))
    specs[2] = pl.BlockSpec((8, cols, chan), lambda i: (last, 0, 0))
    return pl.pallas_call(
        outer_kernel,
        out_shape=whole_shape,
        grid=(1,),
        in_specs=specs,
        out_specs=hbm,
        scratch_shapes=[
            pltpu.VMEM((24, SPAN + 16, chan), F32),
            pltpu.VMEM((10, SPAN, SIZE * 2 * chan), BF16),
            pltpu.VMEM((SPAN, 2 * chan), F32),
            pltpu.VMEM((5, 2, SPAN, chan), F32),
            pltpu.VMEM((7, half_cols, 8 * chan), BF16),
            pltpu.VMEM((SPAN, chan), F32),
            pltpu.VMEM(taps_shape.shape, BF16),
            pltpu.VMEM(coarse_weight.shape, BF16),
            pltpu.VMEM((2, half_cols, 8 * chan), BF16),
            pltpu.VMEM((1, chan), F32),
            pltpu.VMEM((5, half_cols, out_count), BF16),
            pltpu.VMEM((2, 2 * SPAN, 2 * chan), F32),
            pltpu.SemaphoreType.DMA((3,)),
        ],
        input_output_aliases={len(operands) - 1: 0},
        compiler_params=pltpu.CompilerParams(vmem_limit_bytes=64700 * 1024),
        name="outer",
    )(*operands)


def solution(mesh):
    placed = (
        P("lat", "lon", None),
        P("lat", "lon"),
    ) + (P(),) * 13
    return jax.shard_map(
        local, mesh=mesh, in_specs=placed, out_specs=P("lat", "lon", None), check_vma=False
    )
```

profile of v0, /device:TPU:24, one launch (start us, length us, event | category | flops | bytes accessed | tf_op | source)
XLA Modules:
  0.0 46.4 jit_solution(2216601182222315472)
XLA Ops:
  0.0 0.7 %convert_element_type.3 = bf16[32,128]{1,0:T(8,128)(2,1)S(1)} convert(s32[32,128]{1,0:T(8,128)} %land_mask.5) | non-fusion elementwise | flops 4096 | bytes 24576 | tf_op jit(solution)/shard_map/convert_element_type | solution.py:538
  0.7 0.9 %fusion.1 = (bf16[32,4,128]{2,1,0:T(4,128)(2,1)S(1)}, bf16[32,4,128]{2,1,0:T(4,128)(2,1)S(1)}) fusion(bf16[32,128,128]{2,1,0:T(8,128)(2,1)} %feat_high.1), kind=kLoop, calls=%fused_computation.4 | loop fusion | bytes 131072 | tf_op jit(solution)/shard_map/slice | solution.py:543
  1.6 0.1 pad_maximum_fusion
  1.7 6.3 %collective-permute-start.1 = (bf16[40,4,128]{2,1,0:T(4,128)(2,1)S(1)}, bf16[40,4,128]{2,1,0:T(4,128)(2,1)S(1)}, u32[]{:S(2)}, u32[]{:S(2)}) collective-permute-start(bf16[40,4,128]{2,1,0:T(4,128)(2,1)S(1)} %get-tuple-element.21), channel_id=1, source_target_pairs={{1,0},{2,1},{3,2},{4,3},{5,4},{6,5},{7,6},{8,7},{9,8},{10,9},{11,1... | collective-permute-start | bytes 122888 | tf_op jit(solution)/shard_map/ppermute | solution.py:545
  8.0 0.0 collective-permute-start
  8.0 1.0 %fusion = (bf16[4,128,128]{2,1,0:T(8,128)(2,1)S(1)}, bf16[4,128,128]{2,1,0:T(8,128)(2,1)S(1)}) fusion(bf16[32,128,128]{2,1,0:T(8,128)(2,1)} %feat_high.1), kind=kLoop, calls=%fused_computation.3 | loop fusion | bytes 524288 | tf_op jit(solution)/shard_map/slice | solution.py:560
  9.0 0.0 copy-start.2
  9.0 3.7 %prepare.1 = (bf16[256,7168]{1,0:T(8,128)(2,1)}, bf16[640,128]{1,0:T(8,128)(2,1)}) custom-call(f32[7,7,128]{2,1,0:T(8,128)} %dw.3, bf16[512,128]{1,0:T(8,128)(2,1)} %project_w.1, f32[1,128]{1,0:T(1,128)} %bitcast.24), custom_call_target="tpu_custom_call" | custom-call | flops 2000000000 | bytes 4000000 | tf_op jit(solution)/shard_map/prepare/pallas_call | solution.py:587
  12.7 0.1 pad_add_fusion.lat
  12.8 0.0 copy-start.3
  12.8 0.0 collective-permute-done.1.east
  12.8 0.0 copy-start
  12.8 0.8 %collective-permute-done.west = bf16[40,4,128]{2,1,0:T(4,128)(2,1)S(1)} collective-permute-done((bf16[40,4,128]{2,1,0:T(4,128)(2,1)S(1)}, bf16[40,4,128]{2,1,0:T(4,128)(2,1)S(1)}, u32[]{:S(2)}, u32[]{:S(2)}) %collective-permute-start) | collective-permute-done | bytes 40992 | tf_op jit(solution)/shard_map/ppermute | solution.py:544
  13.5 0.0 copy-start.1
  13.5 0.0 copy-done.2
  13.5 0.9 %rims.1 = (bf16[5,144,128]{2,1,0:T(8,128)(2,1)S(1)}, bf16[5,144,128]{2,1,0:T(8,128)(2,1)S(1)}) custom-call(s32[2]{0:T(128)S(1)} %pad_add_fusion.lat, bf16[4,128,128]{2,1,0:T(8,128)(2,1)S(1)} %get-tuple-element.18.feat_low, bf16[4,128,128]{2,1,0:T(8,128)(2,1)S(1)} %get-tuple-element.17.feat_high, bf16[40,4,128]{2,1,0:T(4,128)(2,1)S(1)} %collective-permute-done.west, ...), custom_call_target="tpu_custom_call" | custom-call | tf_op jit(solution)/shard_map/rims/pallas_call | solution.py:552
  14.4 3.2 %collective-permute-start.2 = (bf16[5,144,128]{2,1,0:T(8,128)(2,1)S(1)}, bf16[5,144,128]{2,1,0:T(8,128)(2,1)S(1)}, u32[]{:S(2)}, u32[]{:S(2)}) collective-permute-start(bf16[5,144,128]{2,1,0:T(8,128)(2,1)S(1)} %get-tuple-element.11), channel_id=1, source_target_pairs={{32,0},{0,32},{96,64},{64,96},{160,128},{128,160},{224,192},{192,2... | collective-permute-start | bytes 552968 | tf_op jit(solution)/shard_map/ppermute | solution.py:572
  17.6 2.5 %collective-permute-start.3 = (bf16[5,144,128]{2,1,0:T(8,128)(2,1)S(1)}, bf16[5,144,128]{2,1,0:T(8,128)(2,1)S(1)}, u32[]{:S(2)}, u32[]{:S(2)}) collective-permute-start(bf16[5,144,128]{2,1,0:T(8,128)(2,1)S(1)} %get-tuple-element.12), channel_id=1, source_target_pairs={{0,0},{1,1},{2,2},{3,3},{4,4},{5,5},{6,6},{7,7},{8,8},{9,9},{10,10... | collective-permute-start | bytes 552968 | tf_op jit(solution)/shard_map/ppermute | solution.py:573
  20.1 0.0 copy-done
  20.2 0.0 copy-done.1
  20.2 16.6 %inner.1 = (bf16[16,64,256]{2,1,0:T(8,128)(2,1)}, bf16[2,64,1024]{2,1,0:T(8,128)(2,1)}) custom-call(bf16[32,128,128]{2,1,0:T(8,128)(2,1)} %feat_high.1, bf16[40,4,128]{2,1,0:T(4,128)(2,1)} %copy-done.1, bf16[40,4,128]{2,1,0:T(4,128)(2,1)} %copy-done, s32[32,128]{1,0:T(8,128)} %land_mask.5, f32[1,128]{1,0:T(1,128)} %bitcast.16, f32[1,128]{1,0:T(1,128)} %bitcast.18, ...), custom_call_target="tpu_custom_call" | custom-call | flops 16000000000 | bytes 8000000 | tf_op jit(solution)/shard_map/inner/pallas_call | solution.py:621
  36.7 0.0 copy-done.3
  36.8 0.0 collective-permute-done.2.rim_a
  36.8 0.0 copy-start.4
  36.8 0.0 collective-permute-done.3.rim_b
  36.8 0.0 copy-start.5
  36.8 0.6 %copy-done.4 = bf16[5,144,128]{2,1,0:T(8,128)(2,1)} copy-done((bf16[5,144,128]{2,1,0:T(8,128)(2,1)}, bf16[5,144,128]{2,1,0:T(8,128)(2,1)S(1)}, u32[]{:S(2)}) %copy-start.4) | copy-done | bytes 184344
  37.4 0.1 copy-done.5
  37.5 8.8 %outer.1 = bf16[16,64,256]{2,1,0:T(8,128)(2,1)} custom-call(s32[2]{0:T(128)} %copy-done.3, bf16[32,128,128]{2,1,0:T(8,128)(2,1)} %feat_high.1, bf16[32,128,128]{2,1,0:T(8,128)(2,1)} %feat_high.1, bf16[40,4,128]{2,1,0:T(4,128)(2,1)} %copy-done.1, bf16[40,4,128]{2,1,0:T(4,128)(2,1)} %copy-done, ...), custom_call_target="tpu_custom_call", output_to_operand_aliasing={{}: (23, {})} | custom-call | tf_op jit(solution)/shard_map/outer/pallas_call | solution.py:675
Async XLA Ops:
  1.7 11.1 %collective-permute-start.1 = (bf16[40,4,128]{2,1,0:T(4,128)(2,1)S(1)}, bf16[40,4,128]{2,1,0:T(4,128)(2,1)S(1)}, u32[]{:S(2)}, u32[]{:S(2)}) collective-permute-start(bf16[40,4,128]{2,1,0:T(4,128)(2,1)S(1)} %get-tuple-element.21), channel_id=1, source_target_pairs={{1,0},{2,1},{3,2},{4,3},{5,4},{6,5},{7,6},{8,7},{9,8},{10,9},{11,1... | collective-permute-start | bytes 122888 | tf_op jit(solution)/shard_map/ppermute | solution.py:545
  8.0 5.5 %collective-permute-start = (bf16[40,4,128]{2,1,0:T(4,128)(2,1)S(1)}, bf16[40,4,128]{2,1,0:T(4,128)(2,1)S(1)}, u32[]{:S(2)}, u32[]{:S(2)}) collective-permute-start(bf16[40,4,128]{2,1,0:T(4,128)(2,1)S(1)} %get-tuple-element.22), channel_id=1, source_target_pairs={{0,1},{1,2},{2,3},{3,4},{4,5},{5,6},{6,7},{7,8},{8,9},{9,10},{10,1... | collective-permute-start | bytes 122888 | tf_op jit(solution)/shard_map/ppermute | solution.py:544
  9.0 4.5 %copy-start.2 = (s32[32,128]{1,0:T(8,128)S(1)}, s32[32,128]{1,0:T(8,128)}, u32[]{:S(2)}) copy-start(s32[32,128]{1,0:T(8,128)} %land_mask.5) | copy-start | bytes 49156
  12.8 24.0 %copy-start.3 = (s32[2]{0:T(128)}, s32[2]{0:T(128)S(1)}, u32[]{:S(2)}) copy-start(s32[2]{0:T(128)S(1)} %pad_add_fusion.lat) | copy-start | bytes 28
  12.8 7.4 %copy-start = (bf16[40,4,128]{2,1,0:T(4,128)(2,1)}, bf16[40,4,128]{2,1,0:T(4,128)(2,1)S(1)}, u32[]{:S(2)}) copy-start(bf16[40,4,128]{2,1,0:T(4,128)(2,1)S(1)} %collective-permute-done.1.east) | copy-start | bytes 122884
  13.5 6.6 %copy-start.1 = (bf16[40,4,128]{2,1,0:T(4,128)(2,1)}, bf16[40,4,128]{2,1,0:T(4,128)(2,1)S(1)}, u32[]{:S(2)}) copy-start(bf16[40,4,128]{2,1,0:T(4,128)(2,1)S(1)} %collective-permute-done.west) | copy-start | bytes 122884
  14.4 22.3 %collective-permute-start.2 = (bf16[5,144,128]{2,1,0:T(8,128)(2,1)S(1)}, bf16[5,144,128]{2,1,0:T(8,128)(2,1)S(1)}, u32[]{:S(2)}, u32[]{:S(2)}) collective-permute-start(bf16[5,144,128]{2,1,0:T(8,128)(2,1)S(1)} %get-tuple-element.11), channel_id=1, source_target_pairs={{32,0},{0,32},{96,64},{64,96},{160,128},{128,160},{224,192},{192,2... | collective-permute-start | bytes 552968 | tf_op jit(solution)/shard_map/ppermute | solution.py:572
  17.6 19.2 %collective-permute-start.3 = (bf16[5,144,128]{2,1,0:T(8,128)(2,1)S(1)}, bf16[5,144,128]{2,1,0:T(8,128)(2,1)S(1)}, u32[]{:S(2)}, u32[]{:S(2)}) collective-permute-start(bf16[5,144,128]{2,1,0:T(8,128)(2,1)S(1)} %get-tuple-element.12), channel_id=1, source_target_pairs={{0,0},{1,1},{2,2},{3,3},{4,4},{5,5},{6,6},{7,7},{8,8},{9,9},{10,10... | collective-permute-start | bytes 552968 | tf_op jit(solution)/shard_map/ppermute | solution.py:573
  36.8 0.7 %copy-start.4 = (bf16[5,144,128]{2,1,0:T(8,128)(2,1)}, bf16[5,144,128]{2,1,0:T(8,128)(2,1)S(1)}, u32[]{:S(2)}) copy-start(bf16[5,144,128]{2,1,0:T(8,128)(2,1)S(1)} %collective-permute-done.2.rim_a) | copy-start | bytes 552964
  36.8 0.7 %copy-start.5 = (bf16[5,144,128]{2,1,0:T(8,128)(2,1)}, bf16[5,144,128]{2,1,0:T(8,128)(2,1)S(1)}, u32[]{:S(2)}) copy-start(bf16[5,144,128]{2,1,0:T(8,128)(2,1)S(1)} %collective-permute-done.3.rim_b) | copy-start | bytes 552964
where the time goes:
time: 47.3 us; the launch traced here: 46.4 us
  Pallas kernels  30 us (63%)
  starting transfers between devices  12 us (25%)
  local copies, waits for them, and re-layouts  2.63 us (6%)
  other arithmetic  0.85 us (2%)
  waiting for transfers between devices  0.77 us (2%)
    pallas_call x1, Pallas kernels, local(): pl.pallas_call(inner_kernel, out_shape=(whole_shape, jax.ShapeDtypeStruct...  16.6 us
    pallas_call x1, Pallas kernels, local(): pl.pallas_call(outer_kernel, out_shape=whole_shape, grid=(1,), in_specs=s...  8.85 us
    ppermute x1, starting transfers between devices, local(): east = lax.ppermute(to_west, 'lon', back)  6.3 us
    pallas_call x1, Pallas kernels, local(): pl.pallas_call(prepare_kernel, out_shape=(taps_shape, jax.ShapeDtypeStruc...  3.67 us
    ppermute x1, starting transfers between devices, local(): rim_a = lax.ppermute(swap_a, 'lat', pairs_a)  3.19 us
    ppermute x1, starting transfers between devices, local(): rim_b = lax.ppermute(swap_b, ('lat', 'lon'), pairs_b)  2.54 us
    slice x1, local copies, waits for them, and re-layouts, local(): features[rows - RIM:]  0.99 us
  transfers between devices with their start and end apart: 4, of which 1 were waited for; matrix products, arithmetic and copies ran while one was open for 2% of the time, Pallas kernels for 44%

commit v1 on v0

--- a/solution.py
+++ b/solution.py
@@ -134,15 +134,17 @@
                     ].astype(BF16)
 
 
-def coarse_rows(coarse_in, first, count, coarse_w, coarse_b):
-    total = coarse_b[...]
-    for k in range(2):
-        kernel = jnp.concatenate(
-            [coarse_w[2 * k + h, b] for b in range(4) for h in range(2)], axis=0
-        )
-        window = coarse_in[first + k : first + k + count]
-        total = total + dot(window.reshape(-1, window.shape[2]), kernel)
-    return total.astype(BF16).reshape(count, coarse_in.shape[1], -1)
+def coarse_rows(coarse_in, bands, coarse_w, coarse_b):
+    kernel = jnp.concatenate(
+        [coarse_w[2 * k + h, b] for k in range(2) for b in range(4) for h in range(2)], axis=0
+    )
+    windows = []
+    for first, count in bands:
+        rows = [coarse_in[first + k : first + k + count] for k in range(2)]
+        windows.append(jnp.concatenate(rows, axis=2))
+    window = jnp.concatenate(windows, axis=0)
+    total = dot(window.reshape(-1, window.shape[2]), kernel) + coarse_b[...]
+    return total.astype(BF16).reshape(window.shape[0], coarse_in.shape[1], -1)
 
 
 def own_cells(shifted, at, mid, chan):
@@ -154,42 +156,28 @@
     ]
 
 
-def prepare_kernel(dw, project_w, layer_scale, taps_hbm, project, taps, sems):
-    hid, chan = project_w.shape
-    depth = taps.shape[1] // 4
-
-    def piece(k):
-        cut = slice(k * depth, (k + 1) * depth)
-        return pltpu.make_async_copy(taps.at[:, cut], taps_hbm.at[:, cut], sems.at[k])
-
-    build_taps(dw, taps, lambda k: piece(k).start())
-    scaled = project_w[...].astype(F32) * layer_scale[...]
-    project[:hid] = (0.5 * centred_row(scaled)).astype(BF16)
-    project[hid:] = centring(chan).astype(BF16)
-    for k in range(4):
-        piece(k).wait()
-
-
 def inner_kernel(
     feat,
     west,
     east,
     land_mask,
+    dw,
     dw_bias,
     norm_gain,
     norm_shift,
     expand,
     expand_bias,
-    project,
+    project_w,
     project_b,
     layer_scale,
     out_gain,
     out_shift,
     coarse_b,
-    taps_hbm,
     coarse_w_hbm,
     out,
     edges,
+    project,
+    taps_hbm,
     field,
     shifted,
     norm_buf,
@@ -202,10 +190,19 @@
     sems,
 ):
     rows, cols, chan = feat.shape
-    load_taps = pltpu.make_async_copy(taps_hbm, taps, sems.at[0])
-    load_coarse = pltpu.make_async_copy(coarse_w_hbm, coarse_w, sems.at[1])
-    load_taps.start()
+    depth = taps.shape[1] // 4
+
+    def piece(k):
+        cut = slice(k * depth, (k + 1) * depth)
+        return pltpu.make_async_copy(taps.at[:, cut], taps_hbm.at[:, cut], sems.at[k])
+
+    load_coarse = pltpu.make_async_copy(coarse_w_hbm, coarse_w, sems.at[4])
     load_coarse.start()
+    build_taps(dw, taps, lambda k: piece(k).start())
+    hid = project_w.shape[0]
+    scaled = project_w[...].astype(F32) * layer_scale[...]
+    project[:hid] = (0.5 * centred_row(scaled)).astype(BF16)
+    project[hid:] = centring(chan).astype(BF16)
     field[:, : LEFT - RIM] = jnp.zeros((rows, LEFT - RIM, chan), F32)
     field[:, LEFT + cols + RIM :] = jnp.zeros((rows, SPAN + 16 - LEFT - cols - RIM, chan), F32)
     field[:, LEFT : LEFT + cols] = feat[...].astype(F32)
@@ -232,8 +229,6 @@
     )
     mid = (SIZE // 2) * 2 * chan
 
-    load_taps.wait()
-
     @pl.loop(0, (count - 3) // GROUP)
     def _(group):
         base = group * GROUP
@@ -260,11 +255,11 @@
 
     done = coarse_in.shape[0] - 1
     load_coarse.wait()
-    for first in range(0, done, 4):
-        size = min(4, done - first)
-        out[2 + first : 2 + first + size] = coarse_rows(coarse_in, first, size, coarse_w, coarse_b)
+    out[2 : 2 + done] = coarse_rows(coarse_in, [(0, done)], coarse_w, coarse_b)
     edges[0] = coarse_in[0]
     edges[1] = coarse_in[done]
+    for k in range(4):
+        piece(k).wait()
 
 
 def side_table(land_mask, west, east, marks):
@@ -302,7 +297,7 @@
         at, part = divmod(row, RIM)
         left = west[rows + at].astype(F32)[part : part + 1]
         right = east[rows + at].astype(F32)[part : part + 1]
-        line = land_mask[row : row + 1].astype(F32)
+        line = land_mask[...].astype(F32)[row : row + 1]
         zero = jnp.zeros((SPAN, cols), F32)
         table = (
             jnp.where(deep == place - RIM, line, zero)
@@ -504,8 +499,7 @@
     ]
     cells(streams, refs, norm_buf, coarse_in, average)
     load_coarse.wait()
-    out_buf[:2] = coarse_rows(coarse_in, 0, 2, coarse_w, coarse_b)
-    out_buf[2:5] = coarse_rows(coarse_in, 3, 3, coarse_w, coarse_b)
+    out_buf[...] = coarse_rows(coarse_in, [(0, 2), (3, 3)], coarse_w, coarse_b)
     count = whole.shape[0]
     low_copy = pltpu.make_async_copy(out_buf.at[:2], whole.at[:2], sems.at[0])
     high_copy = pltpu.make_async_copy(out_buf.at[2:5], whole.at[count - 3 : count], sems.at[1])
@@ -557,7 +551,7 @@
         scratch_shapes=[pltpu.VMEM((RIM + 1, SPAN, chan), F32)],
         compiler_params=pltpu.CompilerParams(vmem_limit_bytes=8000 * 1024),
         name="rims",
-    )(lat, features[:RIM], features[rows - RIM :], west, east, land_mask)
+    )(lat, features[:RIM], features[rows - RIM :], west, east, marks)
     pairs_a = [(i ^ 1, i) for i in range(n_lat)]
     pairs_b = []
     for i in range(n_lat):
@@ -584,45 +578,35 @@
         v[None] for v in (out_gain, out_shift, coarse_bias, dw_bias)
     )
     taps_shape = jax.ShapeDtypeStruct((2 * chan, SIZE * 8 * chan), BF16)
-    taps, project = pl.pallas_call(
-        prepare_kernel,
-        out_shape=(taps_shape, jax.ShapeDtypeStruct((hid + chan, chan), BF16)),
-        in_specs=[vmem] * 3,
-        out_specs=(hbm, vmem),
-        scratch_shapes=[
-            pltpu.VMEM(taps_shape.shape, BF16),
-            pltpu.SemaphoreType.DMA((4,)),
-        ],
-        compiler_params=pltpu.CompilerParams(vmem_limit_bytes=58 * 1024 * 1024),
-        cost_estimate=pl.CostEstimate(
-            flops=2_000_000_000, bytes_accessed=4_000_000, transcendentals=0
-        ),
-        name="prepare",
-    )(dw_weight, project_weight, layer_scale)
     operands = (
         features,
         west,
         east,
         land_mask,
+        dw_weight,
         dw_bias,
         norm_gain,
         norm_shift,
         expand_weight,
         expand_bias,
-        project,
+        project_weight,
         project_bias,
         layer_scale,
         out_gain,
         out_shift,
         coarse_bias,
-        taps,
         coarse_weight,
     )
-    whole, edges = pl.pallas_call(
+    whole, edges, project, taps = pl.pallas_call(
         inner_kernel,
-        out_shape=(whole_shape, jax.ShapeDtypeStruct((2, half_cols, 8 * chan), BF16)),
-        in_specs=[vmem] * (len(operands) - 2) + [hbm] * 2,
-        out_specs=(vmem,) * 2,
+        out_shape=(
+            whole_shape,
+            jax.ShapeDtypeStruct((2, half_cols, 8 * chan), BF16),
+            jax.ShapeDtypeStruct((hid + chan, chan), BF16),
+            taps_shape,
+        ),
+        in_specs=[vmem] * (len(operands) - 1) + [hbm],
+        out_specs=(vmem, vmem, vmem, hbm),
         scratch_shapes=[
             pltpu.VMEM((rows, SPAN + 16, chan), F32),
             pltpu.VMEM((inner_pairs + 3, SPAN, SIZE * 2 * chan), BF16),
@@ -633,7 +617,7 @@
             pltpu.VMEM((2, 2 * SPAN, 2 * chan), F32),
             pltpu.VMEM(taps_shape.shape, BF16),
             pltpu.VMEM(coarse_weight.shape, BF16),
-            pltpu.SemaphoreType.DMA((2,)),
+            pltpu.SemaphoreType.DMA((5,)),
         ],
         compiler_params=pltpu.CompilerParams(vmem_limit_bytes=58 * 1024 * 1024),
         cost_estimate=pl.CostEstimate(

time: 47.3 us -> 47.3 us (level)
  waiting for transfers between devices: 0.77 us -> 4.57 us
  Pallas kernels: 30 us -> 26.4 us
    pallas_call x1 -> x0, Pallas kernels: 3.67 us -> none  [local(): pl.pallas_call(prepare_kernel, out_shape=(taps_shape, jax.ShapeDtypeStruc...]
    ppermute x1, waiting for transfers between devices: 0.76 us -> 3.96 us  [local(): west = lax.ppermute(to_east, 'lon', around)]
    ppermute x1, waiting for transfers between devices: 0.01 us -> 0.6 us  [local(): east = lax.ppermute(to_west, 'lon', back)]
  transfers between devices with their start and end apart: 4 -> 4, of which waited for: 1 -> 2; matrix products, arithmetic and copies ran while one was open for 2% -> 2% of each run, Pallas kernels for 44% -> 36%
where the time goes in v1:
time: 47.3 us; the launch traced here: 46.5 us
  Pallas kernels  26.4 us (56%)
  starting transfers between devices  12 us (25%)
  waiting for transfers between devices  4.57 us (10%)
  local copies, waits for them, and re-layouts  2.62 us (6%)
  other arithmetic  0.85 us (2%)
    pallas_call x1, Pallas kernels, local(): pl.pallas_call(inner_kernel, out_shape=(whole_shape, jax.ShapeDtypeStruct...  16.7 us
    pallas_call x1, Pallas kernels, local(): pl.pallas_call(outer_kernel, out_shape=whole_shape, grid=(1,), in_specs=s...  8.85 us
    ppermute x1, starting transfers between devices, local(): east = lax.ppermute(to_west, 'lon', back)  6.3 us
    ppermute x1, waiting for transfers between devices, local(): west = lax.ppermute(to_east, 'lon', around)  3.96 us
    ppermute x1, starting transfers between devices, local(): rim_a = lax.ppermute(swap_a, 'lat', pairs_a)  3.09 us
    ppermute x1, starting transfers between devices, local(): rim_b = lax.ppermute(swap_b, ('lat', 'lon'), pairs_b)  2.6 us
    slice x1, local copies, waits for them, and re-layouts, local(): features[rows - RIM:]  0.99 us
  transfers between devices with their start and end apart: 4, of which 2 were waited for; matrix products, arithmetic and copies ran while one was open for 2% of the time, Pallas kernels for 36%

profile of v1, /device:TPU:24, one launch (start us, length us, event | category | flops | bytes accessed | tf_op | source)
XLA Modules:
  0.0 46.5 jit_solution(7508225940681940081)
XLA Ops:
  0.0 0.7 %convert_element_type.3.land_mask = bf16[32,128]{1,0:T(8,128)(2,1)S(1)} convert(s32[32,128]{1,0:T(8,128)} %land_mask.3) | non-fusion elementwise | flops 4096 | bytes 24576 | tf_op jit(solution)/shard_map/convert_element_type | solution.py:532
  0.7 0.9 %fusion.1 = (bf16[32,4,128]{2,1,0:T(4,128)(2,1)S(1)}, bf16[32,4,128]{2,1,0:T(4,128)(2,1)S(1)}) fusion(bf16[32,128,128]{2,1,0:T(8,128)(2,1)} %feat_high.1), kind=kLoop, calls=%fused_computation.4 | loop fusion | bytes 131072 | tf_op jit(solution)/shard_map/slice | solution.py:537
  1.6 0.1 pad_maximum_fusion
  1.7 6.3 %collective-permute-start.1 = (bf16[40,4,128]{2,1,0:T(4,128)(2,1)S(1)}, bf16[40,4,128]{2,1,0:T(4,128)(2,1)S(1)}, u32[]{:S(2)}, u32[]{:S(2)}) collective-permute-start(bf16[40,4,128]{2,1,0:T(4,128)(2,1)S(1)} %get-tuple-element.21), channel_id=1, source_target_pairs={{1,0},{2,1},{3,2},{4,3},{5,4},{6,5},{7,6},{8,7},{9,8},{10,9},{11,1... | collective-permute-start | bytes 122888 | tf_op jit(solution)/shard_map/ppermute | solution.py:539
  8.0 0.0 collective-permute-start
  8.0 1.0 %fusion = (bf16[4,128,128]{2,1,0:T(8,128)(2,1)S(1)}, bf16[4,128,128]{2,1,0:T(8,128)(2,1)S(1)}) fusion(bf16[32,128,128]{2,1,0:T(8,128)(2,1)} %feat_high.1), kind=kLoop, calls=%fused_computation.3 | loop fusion | bytes 524288 | tf_op jit(solution)/shard_map/slice | solution.py:554
  9.0 0.1 pad_add_fusion.lat
  9.1 0.0 copy-start.2
  9.1 0.6 %collective-permute-done.1.east = bf16[40,4,128]{2,1,0:T(4,128)(2,1)S(1)} collective-permute-done((bf16[40,4,128]{2,1,0:T(4,128)(2,1)S(1)}, bf16[40,4,128]{2,1,0:T(4,128)(2,1)S(1)}, u32[]{:S(2)}, u32[]{:S(2)}) %collective-permute-start.1) | collective-permute-done | bytes 40992 | tf_op jit(solution)/shard_map/ppermute | solution.py:539
  9.7 0.0 copy-start
  9.7 4.0 %collective-permute-done.west = bf16[40,4,128]{2,1,0:T(4,128)(2,1)S(1)} collective-permute-done((bf16[40,4,128]{2,1,0:T(4,128)(2,1)S(1)}, bf16[40,4,128]{2,1,0:T(4,128)(2,1)S(1)}, u32[]{:S(2)}, u32[]{:S(2)}) %collective-permute-start) | collective-permute-done | bytes 40992 | tf_op jit(solution)/shard_map/ppermute | solution.py:538
  13.6 0.0 copy-start.1
  13.6 0.9 %rims.1 = (bf16[5,144,128]{2,1,0:T(8,128)(2,1)S(1)}, bf16[5,144,128]{2,1,0:T(8,128)(2,1)S(1)}) custom-call(s32[2]{0:T(128)S(1)} %pad_add_fusion.lat, bf16[4,128,128]{2,1,0:T(8,128)(2,1)S(1)} %get-tuple-element.18.feat_low, bf16[4,128,128]{2,1,0:T(8,128)(2,1)S(1)} %get-tuple-element.17.feat_high, bf16[40,4,128]{2,1,0:T(4,128)(2,1)S(1)} %collective-permute-done.west, ...), custom_call_target="tpu_custom_call" | custom-call | tf_op jit(solution)/shard_map/rims/pallas_call | solution.py:546
  14.5 3.1 %collective-permute-start.2 = (bf16[5,144,128]{2,1,0:T(8,128)(2,1)S(1)}, bf16[5,144,128]{2,1,0:T(8,128)(2,1)S(1)}, u32[]{:S(2)}, u32[]{:S(2)}) collective-permute-start(bf16[5,144,128]{2,1,0:T(8,128)(2,1)S(1)} %get-tuple-element.11), channel_id=1, source_target_pairs={{32,0},{0,32},{96,64},{64,96},{160,128},{128,160},{224,192},{192,2... | collective-permute-start | bytes 552968 | tf_op jit(solution)/shard_map/ppermute | solution.py:566
  17.6 2.6 %collective-permute-start.3 = (bf16[5,144,128]{2,1,0:T(8,128)(2,1)S(1)}, bf16[5,144,128]{2,1,0:T(8,128)(2,1)S(1)}, u32[]{:S(2)}, u32[]{:S(2)}) collective-permute-start(bf16[5,144,128]{2,1,0:T(8,128)(2,1)S(1)} %get-tuple-element.12), channel_id=1, source_target_pairs={{0,0},{1,1},{2,2},{3,3},{4,4},{5,5},{6,6},{7,7},{8,8},{9,9},{10,10... | collective-permute-start | bytes 552968 | tf_op jit(solution)/shard_map/ppermute | solution.py:567
  20.2 0.0 copy-done
  20.2 0.0 copy-done.1
  20.2 16.7 %inner.1 = (bf16[16,64,256]{2,1,0:T(8,128)(2,1)}, bf16[2,64,1024]{2,1,0:T(8,128)(2,1)}, bf16[640,128]{1,0:T(8,128)(2,1)}, bf16[256,7168]{1,0:T(8,128)(2,1)}) custom-call(bf16[32,128,128]{2,1,0:T(8,128)(2,1)} %feat_high.1, bf16[40,4,128]{2,1,0:T(4,128)(2,1)} %copy-done.1, bf16[40,4,128]{2,1,0:T(4,128)(2,1)} %copy-done, s32[32,128]{1,0:T(8,128)} %land_mask.3, ...), custom_call_target="tpu_custom_call" | custom-call | flops 16000000000 | bytes 8000000 | tf_op jit(solution)/shard_map/inner/pallas_call | solution.py:600
  36.9 0.0 copy-done.2
  36.9 0.0 collective-permute-done.2.rim_a
  36.9 0.0 copy-start.3
  36.9 0.0 collective-permute-done.3.rim_b
  37.0 0.0 copy-start.4
  37.0 0.6 %copy-done.3 = bf16[5,144,128]{2,1,0:T(8,128)(2,1)} copy-done((bf16[5,144,128]{2,1,0:T(8,128)(2,1)}, bf16[5,144,128]{2,1,0:T(8,128)(2,1)S(1)}, u32[]{:S(2)}) %copy-start.3) | copy-done | bytes 184344
  37.6 0.1 copy-done.4
  37.7 8.9 %outer.1 = bf16[16,64,256]{2,1,0:T(8,128)(2,1)} custom-call(s32[2]{0:T(128)} %copy-done.2, bf16[32,128,128]{2,1,0:T(8,128)(2,1)} %feat_high.1, bf16[32,128,128]{2,1,0:T(8,128)(2,1)} %feat_high.1, bf16[40,4,128]{2,1,0:T(4,128)(2,1)} %copy-done.1, bf16[40,4,128]{2,1,0:T(4,128)(2,1)} %copy-done, ...), custom_call_target="tpu_custom_call", output_to_operand_aliasing={{}: (23, {})} | custom-call | tf_op jit(solution)/shard_map/outer/pallas_call | solution.py:659
Async XLA Ops:
  1.7 8.0 %collective-permute-start.1 = (bf16[40,4,128]{2,1,0:T(4,128)(2,1)S(1)}, bf16[40,4,128]{2,1,0:T(4,128)(2,1)S(1)}, u32[]{:S(2)}, u32[]{:S(2)}) collective-permute-start(bf16[40,4,128]{2,1,0:T(4,128)(2,1)S(1)} %get-tuple-element.21), channel_id=1, source_target_pairs={{1,0},{2,1},{3,2},{4,3},{5,4},{6,5},{7,6},{8,7},{9,8},{10,9},{11,1... | collective-permute-start | bytes 122888 | tf_op jit(solution)/shard_map/ppermute | solution.py:539
  8.0 5.6 %collective-permute-start = (bf16[40,4,128]{2,1,0:T(4,128)(2,1)S(1)}, bf16[40,4,128]{2,1,0:T(4,128)(2,1)S(1)}, u32[]{:S(2)}, u32[]{:S(2)}) collective-permute-start(bf16[40,4,128]{2,1,0:T(4,128)(2,1)S(1)} %get-tuple-element.22), channel_id=1, source_target_pairs={{0,1},{1,2},{2,3},{3,4},{4,5},{5,6},{6,7},{7,8},{8,9},{9,10},{10,1... | collective-permute-start | bytes 122888 | tf_op jit(solution)/shard_map/ppermute | solution.py:538
  9.1 27.9 %copy-start.2 = (s32[2]{0:T(128)}, s32[2]{0:T(128)S(1)}, u32[]{:S(2)}) copy-start(s32[2]{0:T(128)S(1)} %pad_add_fusion.lat) | copy-start | bytes 28
  9.7 10.6 %copy-start = (bf16[40,4,128]{2,1,0:T(4,128)(2,1)}, bf16[40,4,128]{2,1,0:T(4,128)(2,1)S(1)}, u32[]{:S(2)}) copy-start(bf16[40,4,128]{2,1,0:T(4,128)(2,1)S(1)} %collective-permute-done.1.east) | copy-start | bytes 122884
  13.6 6.6 %copy-start.1 = (bf16[40,4,128]{2,1,0:T(4,128)(2,1)}, bf16[40,4,128]{2,1,0:T(4,128)(2,1)S(1)}, u32[]{:S(2)}) copy-start(bf16[40,4,128]{2,1,0:T(4,128)(2,1)S(1)} %collective-permute-done.west) | copy-start | bytes 122884
  14.5 22.4 %collective-permute-start.2 = (bf16[5,144,128]{2,1,0:T(8,128)(2,1)S(1)}, bf16[5,144,128]{2,1,0:T(8,128)(2,1)S(1)}, u32[]{:S(2)}, u32[]{:S(2)}) collective-permute-start(bf16[5,144,128]{2,1,0:T(8,128)(2,1)S(1)} %get-tuple-element.11), channel_id=1, source_target_pairs={{32,0},{0,32},{96,64},{64,96},{160,128},{128,160},{224,192},{192,2... | collective-permute-start | bytes 552968 | tf_op jit(solution)/shard_map/ppermute | solution.py:566
  17.6 19.3 %collective-permute-start.3 = (bf16[5,144,128]{2,1,0:T(8,128)(2,1)S(1)}, bf16[5,144,128]{2,1,0:T(8,128)(2,1)S(1)}, u32[]{:S(2)}, u32[]{:S(2)}) collective-permute-start(bf16[5,144,128]{2,1,0:T(8,128)(2,1)S(1)} %get-tuple-element.12), channel_id=1, source_target_pairs={{0,0},{1,1},{2,2},{3,3},{4,4},{5,5},{6,6},{7,7},{8,8},{9,9},{10,10... | collective-permute-start | bytes 552968 | tf_op jit(solution)/shard_map/ppermute | solution.py:567
  36.9 0.7 %copy-start.3 = (bf16[5,144,128]{2,1,0:T(8,128)(2,1)}, bf16[5,144,128]{2,1,0:T(8,128)(2,1)S(1)}, u32[]{:S(2)}) copy-start(bf16[5,144,128]{2,1,0:T(8,128)(2,1)S(1)} %collective-permute-done.2.rim_a) | copy-start | bytes 552964
  37.0 0.7 %copy-start.4 = (bf16[5,144,128]{2,1,0:T(8,128)(2,1)}, bf16[5,144,128]{2,1,0:T(8,128)(2,1)S(1)}, u32[]{:S(2)}) copy-start(bf16[5,144,128]{2,1,0:T(8,128)(2,1)S(1)} %collective-permute-done.3.rim_b) | copy-start | bytes 552964
